TPU v7x, 256 devices: a whole 4x4x8 slice. The times are simulated.
256 devices in a mesh: seq: 64 (over z_lo, x, y), batch: 4 (over z_hi, core).
Axes of the slice: x: 4, y: 4, z: 8 (z_hi: 2, z_lo: 4; z = z_hi * 4 + z_lo), core: 2. Of those that a mesh axis runs over, the one named last changes fastest.
Arguments:
- inputs: bfloat16 [4, 16384, 2048], P('batch', 'seq'), may hold values from -106.50967 to 106.50967
- output_grad: bfloat16 [4, 16384, 2048], P('batch', 'seq'), may hold values from -6 to 6
- norm_gain: float32 [2048], replicated, may hold values from 0.1 to 1.9
- gate_bias: float32 [2048], P('seq'), as said below
- state_in: float32 [4, 2048], P('batch', 'seq'), may hold values from -6 to 6
- w_gate: bfloat16 [2048, 2048], P('seq'), may hold values from -0.44194174 to 0.44194174
- w_cand: bfloat16 [2048, 2048], P('seq'), may hold values from -0.125 to 0.125
- w_out: bfloat16 [2048, 2048], P('seq'), may hold values from -0.125 to 0.125
Outputs:
- layer_out: bfloat16 [4, 16384, 2048], P('batch', 'seq')
- input_grad: bfloat16 [4, 16384, 2048], P('batch', 'seq')
- state_grad: float32 [4, 2048], P('batch', 'seq')
- bias_grad: float32 [2048], P('seq')
Inputs may be any that keep to these rules, and one draw needn't show every extreme that they name: `gate_bias`: every value is at least -ln(16384) - 1.5.
All inputs are finite; a program needn't handle non-finite values.
Results may differ from a plain program's by a relative error of at most 0.013.
Values may be sent and summed in bfloat16 or wider, within the bound.
A program may use at most 128 MiB of HBM per device.

v0:
```python
import jax
import jax.numpy as jnp
from jax import lax
from jax.sharding import PartitionSpec as P

EPSILON = 1e-06


def shifted(values, axis, offset, fill, reverse):
    length = values.shape[axis]
    pad_shape = list(values.shape)
    pad_shape[axis] = offset
    padding = jnp.full(tuple(pad_shape), fill, values.dtype)
    if reverse:
        kept = lax.slice_in_dim(values, offset, length, 1, axis)
        return jnp.concatenate([kept, padding], axis=axis)
    kept = lax.slice_in_dim(values, 0, length - offset, 1, axis)
    return jnp.concatenate([padding, kept], axis=axis)


def shift_scan(keep, drive, axis, reverse):
    length = keep.shape[axis]
    offset = 1
    while offset < length:
        keep_far = shifted(keep, axis, offset, 1.0, reverse)
        drive_far = shifted(drive, axis, offset, 0.0, reverse)
        drive = keep * drive_far + drive
        keep = keep * keep_far
        offset = offset * 2
    return (keep, drive)


def on_device(inputs, output_grad, norm_gain, gate_bias, state_in, w_gate, w_cand, w_out):
    token_rows = inputs[0]
    grad_rows = output_grad[0]
    gate_full, cand_full, out_full = (
        lax.all_gather(w_gate, "seq", axis=0, tiled=True),
        lax.all_gather(w_cand, "seq", axis=0, tiled=True),
        lax.all_gather(w_out, "seq", axis=0, tiled=True),
    )
    residual = token_rows.astype(jnp.float32)
    mean_square = jnp.mean(residual * residual, axis=-1, keepdims=True)
    inverse_rms = lax.rsqrt(mean_square + EPSILON)
    unit_rows = residual * inverse_rms
    normed = (unit_rows * norm_gain).astype(jnp.bfloat16)
    hidden_dim = 0
    contract_model = (((0,), (1,)), ((), ()))
    gate_pre = lax.dot_general(
        gate_full, normed, contract_model, preferred_element_type=jnp.float32
    ).astype(jnp.bfloat16)
    cand_pre = lax.dot_general(
        cand_full, normed, contract_model, preferred_element_type=jnp.float32
    ).astype(jnp.bfloat16)
    back_grads = lax.dot_general(
        out_full, grad_rows, (((1,), (1,)), ((), ())), preferred_element_type=jnp.float32
    ).astype(jnp.bfloat16)
    gate_slab, cand_slab = (
        lax.all_to_all(gate_pre, "seq", split_axis=0, concat_axis=1, tiled=True),
        lax.all_to_all(cand_pre, "seq", split_axis=0, concat_axis=1, tiled=True),
    )
    gate_input = gate_slab.astype(jnp.float32) + gate_bias[:, None]
    update = jax.nn.sigmoid(gate_input)
    retain = jax.nn.sigmoid(-gate_input)
    candidate = cand_slab.astype(jnp.float32)
    initial = state_in[0]
    drive_term = (update * candidate).at[:, 0].add(retain[:, 0] * initial)
    reached, states = shift_scan(retain, drive_term, 1, False)
    state_tok = lax.all_to_all(
        states.astype(jnp.bfloat16), "seq", split_axis=1, concat_axis=0, tiled=True
    )
    back_slab = lax.all_to_all(back_grads, "seq", split_axis=0, concat_axis=1, tiled=True)
    next_retain = jnp.concatenate(
        [retain[:, 1:], jnp.zeros((retain.shape[0], 1), jnp.float32)], axis=1
    )
    tail_keep, carried = shift_scan(next_retain, back_slab.astype(jnp.float32), 1, True)
    state_grad = retain[:, 0] * carried[:, 0]
    earlier_states = jnp.concatenate([initial[:, None], states[:, :-1]], axis=1)
    gate_grad = carried * (candidate - earlier_states) * update * retain
    cand_grad = carried * update
    bias_part = jnp.sum(gate_grad, axis=1)
    gate_tok, cand_tok = (
        lax.all_to_all(
            gate_grad.astype(jnp.bfloat16), "seq", split_axis=1, concat_axis=0, tiled=True
        ),
        lax.all_to_all(
            cand_grad.astype(jnp.bfloat16), "seq", split_axis=1, concat_axis=0, tiled=True
        ),
    )
    contract_hidden = (((hidden_dim,), (0,)), ((), ()))
    layer_rows = (
        residual
        + lax.dot_general(state_tok, out_full, contract_hidden, preferred_element_type=jnp.float32)
    ).astype(jnp.bfloat16)
    contract_back = (((hidden_dim,), (1,)), ((), ()))
    normed_grad = lax.dot_general(
        gate_tok, gate_full, contract_back, preferred_element_type=jnp.float32
    )
    normed_grad = normed_grad + lax.dot_general(
        cand_tok, cand_full, contract_back, preferred_element_type=jnp.float32
    )
    unit_grad = normed_grad * norm_gain
    input_rows = inverse_rms * (
        unit_grad - unit_rows * jnp.mean(unit_grad * unit_rows, axis=-1, keepdims=True)
    )
    token_grad = (grad_rows.astype(jnp.float32) + input_rows).astype(jnp.bfloat16)
    bias_grad = lax.psum(bias_part, "batch")
    return (layer_rows[None], token_grad[None], state_grad[None], bias_grad)


def solution(mesh):
    return jax.shard_map(
        on_device,
        mesh=mesh,
        in_specs=(
            P("batch", "seq", None),
            P("batch", "seq", None),
            P(),
            P("seq"),
            P("batch", "seq"),
            P("seq", None),
            P("seq", None),
            P("seq", None),
        ),
        out_specs=(P("batch", "seq", None), P("batch", "seq", None), P("batch", "seq"), P("seq")),
        check_vma=False,
    )
```

profile of v0, /device:TPU:8, one launch (start us, length us, event | category | flops | bytes accessed | tf_op | source)
XLA Modules:
  0.0 1306.1 jit_solution(2977227251477616313)
XLA Ops:
  10.9 361.7 %all-gather.6.cloned.1.call-done = bf16[2048,2048]{1,0:T(8,128)(2,1)} async-done(((bf16[32,2048]{1,0:T(8,128)(2,1)}), bf16[2048,2048]{1,0:T(8,128)(2,1)}) %all-gather.6.cloned.1.call-update) | async-done | bytes 8388624 | tf_op jit(solution)/shard_map/all_gather | solution.py:38
  372.6 6.1 fusion.6
  380.0 10.6 all-to-all-start.1
  390.6 343.9 %all-gather.4.cloned.1.call-done = bf16[2048,2048]{1,0:T(8,128)(2,1)} async-done(((bf16[32,2048]{1,0:T(8,128)(2,1)}), bf16[2048,2048]{1,0:T(8,128)(2,1)}) %all-gather.4.cloned.1.call-update) | async-done | bytes 8388624 | tf_op jit(solution)/shard_map/all_gather | solution.py:37
  734.5 6.7 fusion.5
  741.2 2.3 copy.31
  743.6 9.9 all-to-all-start
  753.5 340.4 %all-gather.8.cloned.1.call-done = bf16[2048,2048]{1,0:T(8,128)(2,1)} async-done(((bf16[32,2048]{1,0:T(8,128)(2,1)}), bf16[2048,2048]{1,0:T(8,128)(2,1)}) %all-gather.8.cloned.1.call-update) | async-done | bytes 8388624 | tf_op jit(solution)/shard_map/all_gather | solution.py:39
  1093.9 6.7 convolution_convert_fusion
  1100.6 11.7 all-to-all-start.3
  1113.3 1.6 copy.45
  1116.7 13.5 %all-to-all-done.3 = bf16[64,32,256]{2,1,0:T(8,128)(2,1)} async-done(((bf16[64,32,256]{2,1,0:T(8,128)(2,1)}), bf16[64,32,256]{2,1,0:T(8,128)(2,1)}, u32[]{:S(2)}, u32[]{:S(2)}) %all-to-all-start.3) | async-done | bytes 1048608 | tf_op jit(solution)/shard_map/all_to_all | solution.py:71
  1131.9 2.0 slice.294
  1136.8 2.6 fusion.27
  1141.4 4.3 multiply_add_fusion.27
  1148.3 2.5 slice_multiply_fusion
  1151.8 2.1 slice.296
  1153.9 10.3 multiply_add_fusion.11
  1164.2 4.6 multiply_add_fusion.25
  1173.6 9.4 multiply_add_fusion.20
  1202.8 2.9 fusion.24
  1206.8 6.2 all-to-all-start.4
  1213.0 2.8 multiply_convert_fusion
  1217.0 14.3 %all-to-all-done.4 = bf16[32,64,256]{2,0,1:T(8,128)(2,1)} async-done(((bf16[32,64,256]{2,0,1:T(8,128)(2,1)}), bf16[32,64,256]{2,0,1:T(8,128)(2,1)}, u32[]{:S(2)}, u32[]{:S(2)}) %all-to-all-start.4) | async-done | bytes 1048608 | tf_op jit(solution)/shard_map/all_to_all | solution.py:82
  1231.2 6.2 all-to-all-start.5
  1238.6 16.1 %psum.7 = f32[32]{0:T(128)} all-reduce(f32[32]{0:T(128)S(1)} %get-tuple-element.16), channel_id=1, replica_groups=mesh['seq'=64,'batch'=4] {'batch'}, use_global_device_ids=true, to_apply=%region_4.0 | all-reduce | flops 32 | bytes 256 | tf_op jit(solution)/shard_map/psum | solution.py:106
  1256.1 11.1 all-to-all-start.2
  1267.2 6.2 fusion.28
  1273.4 6.5 fusion.9
  1280.0 1.6 fusion.18
  1281.6 10.9 all-to-all-done.2
  1292.5 6.7 fusion.7
  (136 shorter events, 46.9 us)
Async XLA Ops:
  7.2 365.4 %all-gather.6.cloned.1.call-start = ((), (), s32[]{:S(2)}) async-start(), calls=%async_computation.7 | async-start | bytes 8519680 | tf_op jit(solution)/shard_map/all_gather | solution.py:38
  7.9 726.6 %all-gather.4.cloned.1.call-start = ((), (), s32[]{:S(2)}) async-start(), calls=%async_computation.6 | async-start | bytes 8519680 | tf_op jit(solution)/shard_map/all_gather | solution.py:37
  8.6 1085.2 %all-gather.8.cloned.1.call-start = ((), (), s32[]{:S(2)}) async-start(), calls=%async_computation.8 | async-start | bytes 8519680 | tf_op jit(solution)/shard_map/all_gather | solution.py:39
  10.9 723.6 %copy-start.20 = (f32[256]{0:T(256)}, f32[256]{0:T(256)S(1)}, u32[]{:S(2)}) copy-start(f32[256]{0:T(256)S(1)} %add_rsqrt_fusion) | copy-start | bytes 3076
  378.7 355.8 %copy-start.12 = (bf16[1,256,2048]{2,1,0:T(8,128)(2,1)S(1)}, bf16[1,256,2048]{2,1,0:T(8,128)(2,1)}, u32[]{:S(2)}) copy-start(bf16[1,256,2048]{2,1,0:T(8,128)(2,1)} %param.10) | copy-start | bytes 3145732
  378.7 355.8 %copy-start.23 = (f32[2048]{0:T(1024)S(1)}, f32[2048]{0:T(1024)}, u32[]{:S(2)}) copy-start(f32[2048]{0:T(1024)} %param.12) | copy-start | bytes 24580
  380.0 363.5 %all-to-all-start.1 = ((bf16[64,32,256]{2,1,0:T(8,128)(2,1)}), bf16[64,32,256]{2,1,0:T(8,128)(2,1)S(1)}, u32[]{:S(2)}, u32[]{:S(2)}) async-start(bf16[64,32,256]{2,1,0:T(8,128)(2,1)} %bitcast.6), calls=%async_computation.1 | async-start | bytes 2097152 | tf_op jit(solution)/shard_map/all_to_all | solution.py:59
  741.2 352.6 %copy-start.17 = (bf16[1,256,2048]{2,1,0:T(8,128)(2,1)S(1)}, bf16[1,256,2048]{2,1,0:T(8,128)(2,1)}, u32[]{:S(2)}) copy-start(bf16[1,256,2048]{2,1,0:T(8,128)(2,1)} %param.11) | copy-start | bytes 3145732
  743.6 357.0 %all-to-all-start = ((bf16[64,32,256]{2,1,0:T(8,128)(2,1)}), bf16[64,32,256]{2,1,0:T(8,128)(2,1)S(1)}, u32[]{:S(2)}, u32[]{:S(2)}) async-start(bf16[64,32,256]{2,1,0:T(8,128)(2,1)} %bitcast.3), calls=%async_computation | async-start | bytes 2097152 | tf_op jit(solution)/shard_map/all_to_all | solution.py:58
  1100.6 11.7 copy-start.22
  1100.6 11.8 copy-start.15
  1100.6 29.6 %all-to-all-start.3 = ((bf16[64,32,256]{2,1,0:T(8,128)(2,1)}), bf16[64,32,256]{2,1,0:T(8,128)(2,1)}, u32[]{:S(2)}, u32[]{:S(2)}) async-start(bf16[64,32,256]{2,1,0:T(8,128)(2,1)} %bitcast.110), calls=%async_computation.3 | async-start | bytes 2097152 | tf_op jit(solution)/shard_map/all_to_all | solution.py:71
  1113.3 1.6 copy-start.16
  1131.8 2.1 copy-start.5
  1131.9 3.1 copy-start.2
  1131.9 3.7 copy-start.8
  1131.9 3.7 copy-start.19
  1136.8 2.6 copy-start.4
  1141.4 4.3 copy-start
  1145.7 2.2 copy-start.14
  1147.9 3.5 copy-start.1
  1151.8 2.1 copy-start.7
  1186.4 1.6 copy-start.10
  1200.6 1.6 copy-start.3
  1200.6 2.2 copy-start.9
  1206.8 24.5 %all-to-all-start.4 = ((bf16[32,64,256]{2,0,1:T(8,128)(2,1)}), bf16[32,64,256]{2,0,1:T(8,128)(2,1)}, u32[]{:S(2)}, u32[]{:S(2)}) async-start(bf16[32,64,256]{2,0,1:T(8,128)(2,1)} %bitcast.107), calls=%async_computation.4 | async-start | bytes 2097152 | tf_op jit(solution)/shard_map/all_to_all | solution.py:82
  1231.2 24.8 %all-to-all-start.5 = ((bf16[32,64,256]{2,0,1:T(8,128)(2,1)}), bf16[32,64,256]{2,0,1:T(8,128)(2,1)}, u32[]{:S(2)}, u32[]{:S(2)}) async-start(bf16[32,64,256]{2,0,1:T(8,128)(2,1)} %bitcast.106), calls=%async_computation.5 | async-start | bytes 2097152 | tf_op jit(solution)/shard_map/all_to_all | solution.py:85
  1256.1 36.4 %all-to-all-start.2 = ((bf16[32,64,256]{2,0,1:T(8,128)(2,1)}), bf16[32,64,256]{2,0,1:T(8,128)(2,1)S(1)}, u32[]{:S(2)}, u32[]{:S(2)}) async-start(bf16[32,64,256]{2,0,1:T(8,128)(2,1)} %bitcast.105), calls=%async_computation.2 | async-start | bytes 2097152 | tf_op jit(solution)/shard_map/all_to_all | solution.py:68
  1267.2 6.2 copy-start.13
  1267.2 6.2 copy-start.21
  1267.2 6.2 copy-start.24
  1273.4 6.5 copy-start.18
  (2 other events, 3.2 us)
Sparse Core Ops, SparseCore 0:
  9.8 362.7 all-gather.5
  374.4 360.0 all-gather.3
  736.3 357.5 all-gather.7
where the time goes:
time: 1310 us
  waiting for transfers between devices  1090 us (83%)
  other arithmetic  57.8 us (4%)
  starting transfers between devices  55.8 us (4%)
  matrix products  39 us (3%)
  local copies, waits for them, and re-layouts  36 us (3%)
  blocking collectives  16.1 us (1%)
  between operations  14.9 us (1%)
    all_gather x1, waiting for transfers between devices, on_device(): lax.all_gather(w_cand, 'seq', axis=0, tiled=True)  362 us
    all_gather x1, waiting for transfers between devices, on_device(): lax.all_gather(w_gate, 'seq', axis=0, tiled=True)  344 us
    all_gather x1, waiting for transfers between devices, on_device(): lax.all_gather(w_out, 'seq', axis=0, tiled=True)  340 us
    add x25, other arithmetic, shift_scan(): drive = keep * drive_far + drive  40.3 us
  transfers between devices with their start and end apart: 9, of which 6 were waited for; matrix products, arithmetic and copies ran while one was open for 4% of the time, Pallas kernels for 0%

commit v1 on v0

--- a/solution.py
+++ b/solution.py
@@ -2,8 +2,17 @@
 import jax.numpy as jnp
 from jax import lax
 from jax.sharding import PartitionSpec as P
+from jax.lax import all_to_all, psum
 
 EPSILON = 1e-06
+
+
+def manage_turns(m, bus_axis):
+    met_up = tuple((m for _ in range(psum(1, axis_name=bus_axis))))
+    long_array = jnp.stack(met_up)
+    f_next = all_to_all(long_array, bus_axis, 0, 0)
+    d_next = jnp.concatenate(f_next, axis=0)
+    return d_next
 
 
 def shifted(values, axis, offset, fill, reverse):
@@ -34,7 +43,7 @@
     token_rows = inputs[0]
     grad_rows = output_grad[0]
     gate_full, cand_full, out_full = (
-        lax.all_gather(w_gate, "seq", axis=0, tiled=True),
+        manage_turns(w_gate, "seq"),
         lax.all_gather(w_cand, "seq", axis=0, tiled=True),
         lax.all_gather(w_out, "seq", axis=0, tiled=True),
     )

time: 1310 us -> 1060 us (0.81)
  waiting for transfers between devices: 1090 us -> 822 us
    all_gather x1 -> x0, waiting for transfers between devices: 344 us -> none  [on_device(): lax.all_gather(w_gate, 'seq', axis=0, tiled=True)]
    all_gather x1, waiting for transfers between devices: 362 us -> 427 us  [on_device(): lax.all_gather(w_cand, 'seq', axis=0, tiled=True)]
  transfers between devices with their start and end apart: 9 -> 9, of which waited for: 6 -> 6; matrix products, arithmetic and copies ran while one was open for 4% -> 5% of each run, Pallas kernels for 0% -> 0%
where the time goes in v1:
time: 1060 us; the launch traced here: 1050 us
  waiting for transfers between devices  822 us (78%)
  starting transfers between devices  63.3 us (6%)
  other arithmetic  56.4 us (5%)
  local copies, waits for them, and re-layouts  40.4 us (4%)
  matrix products  38.6 us (4%)
  blocking collectives  16.3 us (2%)
  between operations  15.2 us (1%)
    all_gather x1, waiting for transfers between devices, on_device(): lax.all_gather(w_cand, 'seq', axis=0, tiled=True)  427 us
    all_gather x1, waiting for transfers between devices, on_device(): lax.all_gather(w_out, 'seq', axis=0, tiled=True)  348 us
    add x25, other arithmetic, shift_scan(): drive = keep * drive_far + drive  40.4 us
  transfers between devices with their start and end apart: 9, of which 6 were waited for; matrix products, arithmetic and copies ran while one was open for 5% of the time, Pallas kernels for 0%

profile of v1, /device:TPU:8, one launch (start us, length us, event | category | flops | bytes accessed | tf_op | source)
XLA Modules:
  0.0 1052.6 jit_solution(13215187332507321735)
XLA Ops:
  7.9 5.2 stack.2
  13.1 12.3 %all-to-all-start = ((bf16[64,32,2048]{2,1,0:T(8,128)(2,1)}), bf16[64,32,2048]{2,1,0:T(8,128)(2,1)}, u32[]{:S(2)}, u32[]{:S(2)}) async-start(bf16[64,32,2048]{2,1,0:T(8,128)(2,1)} %stack.2), calls=%async_computation | async-start | bytes 16777216 | tf_op jit(solution)/shard_map/all_to_all | solution.py:13
  26.5 426.6 %all-gather.3.cloned.1.call-done = bf16[2048,2048]{1,0:T(8,128)(2,1)} async-done(((bf16[32,2048]{1,0:T(8,128)(2,1)}), bf16[2048,2048]{1,0:T(8,128)(2,1)}) %all-gather.3.cloned.1.call-update) | async-done | bytes 8388624 | tf_op jit(solution)/shard_map/all_gather | solution.py:47
  453.2 5.8 fusion.9
  460.3 9.9 all-to-all-start.2
  470.1 348.4 %all-gather.5.cloned.1.call-done = bf16[2048,2048]{1,0:T(8,128)(2,1)} async-done(((bf16[32,2048]{1,0:T(8,128)(2,1)}), bf16[2048,2048]{1,0:T(8,128)(2,1)}) %all-gather.5.cloned.1.call-update) | async-done | bytes 8388624 | tf_op jit(solution)/shard_map/all_gather | solution.py:48
  818.5 6.7 convolution_convert_fusion
  825.3 11.0 %all-to-all-start.4 = ((bf16[64,32,256]{2,1,0:T(8,128)(2,1)}), bf16[64,32,256]{2,1,0:T(8,128)(2,1)S(1)}, u32[]{:S(2)}, u32[]{:S(2)}) async-start(bf16[64,32,256]{2,1,0:T(8,128)(2,1)} %bitcast.140), calls=%async_computation.4 | async-start | bytes 2097152 | tf_op jit(solution)/shard_map/all_to_all | solution.py:80
  836.4 6.7 fusion.8
  843.1 2.3 copy.31
  845.4 9.1 all-to-all-done.4
  854.5 6.7 all-to-all-start.1
  866.3 12.9 %all-to-all-done.1 = bf16[64,32,256]{2,1,0:T(8,128)(2,1)} async-done(((bf16[64,32,256]{2,1,0:T(8,128)(2,1)}), bf16[64,32,256]{2,1,0:T(8,128)(2,1)}, u32[]{:S(2)}, u32[]{:S(2)}) %all-to-all-start.1) | async-done | bytes 1048608 | tf_op jit(solution)/shard_map/all_to_all | solution.py:67
  880.9 2.1 copy-done.8
  884.3 2.6 fusion.37
  888.9 4.3 multiply_add_fusion.27
  895.8 2.5 slice_multiply_fusion
  899.3 2.1 slice.296
  901.4 10.3 multiply_add_fusion.11
  911.7 4.6 multiply_add_fusion.25
  921.1 9.4 multiply_add_fusion.20
  950.3 2.8 fusion.34
  954.2 6.2 all-to-all-start.5
  960.4 2.8 multiply_convert_fusion
  964.5 14.2 %all-to-all-done.5 = bf16[32,64,256]{2,0,1:T(8,128)(2,1)} async-done(((bf16[32,64,256]{2,0,1:T(8,128)(2,1)}), bf16[32,64,256]{2,0,1:T(8,128)(2,1)}, u32[]{:S(2)}, u32[]{:S(2)}) %all-to-all-start.5) | async-done | bytes 1048608 | tf_op jit(solution)/shard_map/all_to_all | solution.py:91
  978.6 6.2 all-to-all-start.6
  986.0 16.3 %psum.7 = f32[32]{0:T(128)} all-reduce(f32[32]{0:T(128)S(1)} %get-tuple-element.16), channel_id=1, replica_groups=mesh['seq'=64,'batch'=4] {'batch'}, use_global_device_ids=true, to_apply=%region_4.0 | all-reduce | flops 32 | bytes 256 | tf_op jit(solution)/shard_map/psum | solution.py:115
  1003.6 10.8 %all-to-all-start.3 = ((bf16[32,64,256]{2,0,1:T(8,128)(2,1)}), bf16[32,64,256]{2,0,1:T(8,128)(2,1)S(1)}, u32[]{:S(2)}, u32[]{:S(2)}) async-start(bf16[32,64,256]{2,0,1:T(8,128)(2,1)} %bitcast.135), calls=%async_computation.3 | async-start | bytes 2097152 | tf_op jit(solution)/shard_map/all_to_all | solution.py:77
  1014.5 6.2 fusion.38
  1020.7 6.5 fusion.12
  1028.8 9.8 all-to-all-done.3
  1038.6 6.7 fusion.10
  (136 shorter events, 47.2 us)
Async XLA Ops:
  7.2 446.0 %all-gather.3.cloned.1.call-start = ((), (), s32[]{:S(2)}) async-start(), calls=%async_computation.7 | async-start | bytes 8519680 | tf_op jit(solution)/shard_map/all_gather | solution.py:47
  13.1 13.1 %copy-start.12 = (bf16[1,256,2048]{2,1,0:T(8,128)(2,1)S(1)}, bf16[1,256,2048]{2,1,0:T(8,128)(2,1)}, u32[]{:S(2)}) copy-start(bf16[1,256,2048]{2,1,0:T(8,128)(2,1)} %param.10) | copy-start | bytes 3145732
  13.1 440.0 %copy-start.23 = (f32[2048]{0:T(1024)S(1)}, f32[2048]{0:T(1024)}, u32[]{:S(2)}) copy-start(f32[2048]{0:T(1024)} %param.12) | copy-start | bytes 24580
  13.1 447.1 %all-to-all-start = ((bf16[64,32,2048]{2,1,0:T(8,128)(2,1)}), bf16[64,32,2048]{2,1,0:T(8,128)(2,1)}, u32[]{:S(2)}, u32[]{:S(2)}) async-start(bf16[64,32,2048]{2,1,0:T(8,128)(2,1)} %stack.2), calls=%async_computation | async-start | bytes 16777216 | tf_op jit(solution)/shard_map/all_to_all | solution.py:13
  25.5 793.1 %all-gather.5.cloned.1.call-start = ((), (), s32[]{:S(2)}) async-start(), calls=%async_computation.8 | async-start | bytes 8519680 | tf_op jit(solution)/shard_map/all_gather | solution.py:48
  26.5 809.8 %copy-start.20 = (f32[256]{0:T(256)}, f32[256]{0:T(256)S(1)}, u32[]{:S(2)}) copy-start(f32[256]{0:T(256)S(1)} %add_rsqrt_fusion) | copy-start | bytes 3076
  458.9 359.6 %copy-start.17 = (bf16[1,256,2048]{2,1,0:T(8,128)(2,1)S(1)}, bf16[1,256,2048]{2,1,0:T(8,128)(2,1)}, u32[]{:S(2)}) copy-start(bf16[1,256,2048]{2,1,0:T(8,128)(2,1)} %param.11) | copy-start | bytes 3145732
  460.3 365.0 %all-to-all-start.2 = ((bf16[64,32,256]{2,1,0:T(8,128)(2,1)}), bf16[64,32,256]{2,1,0:T(8,128)(2,1)S(1)}, u32[]{:S(2)}, u32[]{:S(2)}) async-start(bf16[64,32,256]{2,1,0:T(8,128)(2,1)} %bitcast.7), calls=%async_computation.2 | async-start | bytes 2097152 | tf_op jit(solution)/shard_map/all_to_all | solution.py:68
  825.3 29.2 %all-to-all-start.4 = ((bf16[64,32,256]{2,1,0:T(8,128)(2,1)}), bf16[64,32,256]{2,1,0:T(8,128)(2,1)S(1)}, u32[]{:S(2)}, u32[]{:S(2)}) async-start(bf16[64,32,256]{2,1,0:T(8,128)(2,1)} %bitcast.140), calls=%async_computation.4 | async-start | bytes 2097152 | tf_op jit(solution)/shard_map/all_to_all | solution.py:80
  843.1 18.1 %copy-start.22 = (f32[1,32]{1,0:T(1,128)S(1)}, f32[1,32]{1,0:T(1,128)}, u32[]{:S(2)}) copy-start(f32[1,32]{1,0:T(1,128)} %param.14) | copy-start | bytes 388
  854.5 6.8 copy-start.15
  854.5 24.7 %all-to-all-start.1 = ((bf16[64,32,256]{2,1,0:T(8,128)(2,1)}), bf16[64,32,256]{2,1,0:T(8,128)(2,1)}, u32[]{:S(2)}, u32[]{:S(2)}) async-start(bf16[64,32,256]{2,1,0:T(8,128)(2,1)} %bitcast.4), calls=%async_computation.1 | async-start | bytes 2097152 | tf_op jit(solution)/shard_map/all_to_all | solution.py:67
  864.2 2.1 copy-start.5
  880.7 2.4 copy-start.8
  880.7 2.3 copy-start.19
  880.9 3.3 copy-start.2
  884.2 2.6 copy-start.4
  888.9 4.3 copy-start
  893.2 1.6 copy-start.6
  893.2 2.2 copy-start.14
  895.4 3.5 copy-start.1
  899.3 2.1 copy-start.7
  933.9 1.6 copy-start.10
  948.1 1.6 copy-start.3
  948.1 2.2 copy-start.9
  954.2 24.5 %all-to-all-start.5 = ((bf16[32,64,256]{2,0,1:T(8,128)(2,1)}), bf16[32,64,256]{2,0,1:T(8,128)(2,1)}, u32[]{:S(2)}, u32[]{:S(2)}) async-start(bf16[32,64,256]{2,0,1:T(8,128)(2,1)} %bitcast.137), calls=%async_computation.5 | async-start | bytes 2097152 | tf_op jit(solution)/shard_map/all_to_all | solution.py:91
  978.6 25.0 %all-to-all-start.6 = ((bf16[32,64,256]{2,0,1:T(8,128)(2,1)}), bf16[32,64,256]{2,0,1:T(8,128)(2,1)}, u32[]{:S(2)}, u32[]{:S(2)}) async-start(bf16[32,64,256]{2,0,1:T(8,128)(2,1)} %bitcast.136), calls=%async_computation.6 | async-start | bytes 2097152 | tf_op jit(solution)/shard_map/all_to_all | solution.py:94
  1003.6 35.0 %all-to-all-start.3 = ((bf16[32,64,256]{2,0,1:T(8,128)(2,1)}), bf16[32,64,256]{2,0,1:T(8,128)(2,1)S(1)}, u32[]{:S(2)}, u32[]{:S(2)}) async-start(bf16[32,64,256]{2,0,1:T(8,128)(2,1)} %bitcast.135), calls=%async_computation.3 | async-start | bytes 2097152 | tf_op jit(solution)/shard_map/all_to_all | solution.py:77
  1014.4 6.2 copy-start.13
  1014.4 6.2 copy-start.21
  1014.5 6.2 copy-start.24
  1020.7 6.5 copy-start.18
  (2 other events, 3.1 us)
Sparse Core Ops, SparseCore 0:
  9.8 443.3 all-gather.2
  455.0 363.5 all-gather.4
